TPU v7x, 32 devices: a whole 2x2x4 slice. The times are simulated.
32 devices in a mesh: sector: 4 (over z), group: 8 (over y, x, core).
Axes of the slice: x: 2, y: 2, z: 4, core: 2. Of those that a mesh axis runs over, the one named last changes fastest.
Arguments:
- spectrum: float32 [1152, 128, 512], P('group', None, 'sector'), may hold values from 0.1 to 2
- land_mask: int32 [128, 512], P(None, 'sector'), may hold values 0 or 1
- wind_field: float32 [2, 128, 512], P(None, 'group', 'sector'), may hold values from -3 to 3
- assignment: int32 [1152], replicated, may hold values from 0 to 1151, each once
- courant: float32 [32], replicated, may hold values from 0.3 to 0.65
- growth: float32 [32], replicated, may hold values from 0.1 to 0.5
- whitecap: float32 [32], replicated, may hold values from 0.2 to 1
- weights: float32 [32], replicated, may hold values from 0.5 to 5
- spread: float32 [32, 36, 36], replicated, may hold values from -1 to 1
Outputs:
- updated: float32 [1152, 128, 512], P('group', None, 'sector')
Inputs may be any that keep to these rules, and one draw needn't show every extreme that they name: `assignment`: each component number appears exactly once.
All inputs are finite; a program needn't handle non-finite values. No bound on the sum of `land_mask` on one device may be relied on, other than what follows from the above.
Results may differ from a plain program's by a relative error of at most 0.00007.
Values sent between devices are 32-bit elements; how exact they have to be, the bound alone decides.
No kernel may reach another device: no remote copies, remote signals or barrier semaphores. Data moves between devices by JAX's collectives and lax.ppermute only.
A program may use at most 128 MiB of HBM per device.

v0:
```python
import math
import jax
import jax.numpy as jnp
from jax import lax
from jax.sharding import PartitionSpec as P

DIRS = 36
FREQ = 32
SUBSTEPS = 6
LAT = 128


def extended(cells, sides, width):
    for axis, dim in sides:
        count = lax.axis_size(axis)
        head = lax.slice_in_dim(cells, 0, width, axis=dim)
        tail = lax.slice_in_dim(cells, cells.shape[dim] - width, cells.shape[dim], axis=dim)
        cells = jnp.concatenate(
            [
                lax.ppermute(tail, axis, [(i, (i + 1) % count) for i in range(count)]),
                cells,
                lax.ppermute(head, axis, [((i + 1) % count, i) for i in range(count)]),
            ],
            axis=dim,
        )
    return cells


def freq_onehot(frequency):
    return (frequency[:, None] == jnp.arange(FREQ)[None, :]).astype(jnp.float32)


def flow_terms(kinds, courant):
    direction = kinds % DIRS
    frequency = kinds // DIRS
    angles = (direction.astype(jnp.float32) + 0.5) * (2.0 * math.pi / DIRS)
    speeds = jnp.dot(freq_onehot(frequency), courant, precision=lax.Precision.HIGHEST)
    latitude = (jnp.arange(LAT).astype(jnp.float32) + 0.5 - LAT / 2) * (math.pi / 2160.0)
    flow_x = speeds[:, None] * jnp.cos(angles)[:, None] / jnp.cos(latitude)[None, :]
    flow_y = speeds * jnp.sin(angles)
    return (flow_x, flow_y)


def combine(centre, from_west, from_east, rates):
    keep_rate, east_rate, west_rate, north_rate, south_rate = rates
    from_south = jnp.pad(centre[:, :-1], ((0, 0), (1, 0), (0, 0)))
    from_north = jnp.pad(centre[:, 1:], ((0, 0), (0, 1), (0, 0)))
    return (
        keep_rate * centre
        + east_rate * from_west
        + west_rate * from_east
        + north_rate * from_south
        + south_rate * from_north
    )


def propagate(wave, flow_x, flow_y, sea_mask):
    rates = (
        1.0 - jnp.abs(flow_x)[:, :, None] - jnp.abs(flow_y)[:, None, None],
        jnp.maximum(flow_x, 0.0)[:, :, None],
        jnp.maximum(-flow_x, 0.0)[:, :, None],
        jnp.maximum(flow_y, 0.0)[:, None, None],
        jnp.maximum(-flow_y, 0.0)[:, None, None],
    )
    for substep in range(SUBSTEPS):
        padded = extended(wave, (("sector", 2),), 1)
        wave = combine(wave, padded[:, :, :-2], padded[:, :, 2:], rates) * sea_mask[None]
    return wave


def local(spectrum, land_mask, wind_field, assignment, courant, growth, whitecap, weights, spread):
    member = lax.axis_index("group")
    comps_dev = spectrum.shape[0]
    lon_local = spectrum.shape[2]
    all_comps = assignment.shape[0]
    rows_dev = wind_field.shape[1]
    sea_mask = land_mask.astype(jnp.float32)
    kinds = lax.dynamic_slice_in_dim(assignment, member * comps_dev, comps_dev, 0)
    flow_x, flow_y = flow_terms(kinds, courant)
    moved = lax.all_to_all(
        propagate(spectrum, flow_x, flow_y, sea_mask),
        "group",
        split_axis=1,
        concat_axis=0,
        tiled=True,
    )
    points = rows_dev * lon_local
    energy = moved.reshape(all_comps, points)
    sea_rows = lax.dynamic_slice_in_dim(sea_mask, member * rows_dev, rows_dev, 0).reshape(points)
    winds = wind_field.reshape(2, points)
    direction = assignment % DIRS
    frequency = assignment // DIRS
    angles = (direction.astype(jnp.float32) + 0.5) * (2.0 * math.pi / DIRS)
    per_freq = jnp.stack((growth, whitecap, weights), axis=1)
    picked = jnp.dot(freq_onehot(frequency), per_freq, precision=lax.Precision.HIGHEST)
    kind_onehot = (assignment[:, None] == jnp.arange(all_comps)[None, :]).astype(jnp.float32)
    picked_rows = jnp.dot(
        kind_onehot, spread.reshape(FREQ * DIRS, DIRS), precision=lax.Precision.HIGHEST
    )
    dir_onehot = (jnp.arange(DIRS)[:, None] == direction[None, :]).astype(jnp.float32)
    same_freq = (frequency[:, None] == frequency[None, :]).astype(jnp.float32)
    coupling = jnp.dot(picked_rows, dir_onehot, precision=lax.Precision.HIGHEST) * same_freq
    loading = jnp.sum(picked[:, 2][:, None] * energy, axis=0) / all_comps
    drive = (
        jnp.cos(angles)[:, None] * winds[0][None, :] + jnp.sin(angles)[:, None] * winds[1][None, :]
    )
    exponent = (
        picked[:, 0][:, None] * jnp.maximum(drive, 0.0)
        - picked[:, 1][:, None] * (loading / (1.0 + loading))[None, :]
    )
    mixed = jnp.dot(coupling, energy, precision=lax.Precision.HIGHEST)
    renewed = (energy * jnp.exp(exponent) + 0.5 * mixed) * sea_rows[None, :]
    return lax.all_to_all(
        renewed.reshape(all_comps, rows_dev, lon_local),
        "group",
        split_axis=0,
        concat_axis=1,
        tiled=True,
    )


def solution(mesh):
    in_specs = (
        P("group", None, "sector"),
        P(None, "sector"),
        P(None, "group", "sector"),
        P(),
        P(),
        P(),
        P(),
        P(),
        P(),
    )
    out_specs = P("group", None, "sector")
    return jax.shard_map(local, mesh=mesh, in_specs=in_specs, out_specs=out_specs, check_vma=False)
```

profile of v0, /device:TPU:0, one launch (start us, length us, event | category | flops | bytes accessed | tf_op | source)
XLA Modules:
  0.0 494.8 jit_solution(8796984362894581755)
XLA Ops:
  0.0 9.6 %copy.15 = f32[144,128,128]{1,0,2:T(8,128)} copy(f32[144,128,128]{2,1,0:T(8,128)} %param.9) | data formatting | bytes 18874368 | tf_op args[0]
  9.6 0.9 fusion.83
  10.5 3.1 collective-permute-start
  13.6 2.1 collective-permute-start.1
  15.8 0.0 copy-start.4
  15.8 0.0 copy-start.3
  15.8 14.2 %fusion.82 = (f32[144,127,128]{1,0,2:T(8,128)}, f32[144,127,128]{1,0,2:T(8,128)}) fusion(f32[144,128,128]{1,0,2:T(8,128)} %copy.15), kind=kLoop, calls=%fused_computation.122 | loop fusion | bytes 37453824 | tf_op jit(solution)/shard_map/slice | solution.py:46
  30.0 0.1 and_select_fusion.1
  30.1 0.2 fusion.55
  30.3 0.2 fusion.70
  30.6 0.1 subtract_subtract_fusion
  30.7 0.1 copy.22
  30.8 0.0 collective-permute-done
  30.8 0.0 collective-permute-done.1
  30.8 16.4 %fusion.43 = f32[144,128,128]{1,0,2:T(8,128)S(1)} fusion(f32[144,128,1]{1,0,2:T(8,128)S(1)} %collective-permute-done.1, f32[144,128,128]{1,0,2:T(8,128)} %copy.15, f32[144,128,1]{1,0,2:T(8,128)S(1)} %collective-permute-done, f32[144,127,128]{1,0,2:T(8,128)} %get-tuple-element.31, f32[144,127,128]{1,0,2:T(8,128)} %get-tuple-element.30, ...), kind=kLoop, calls=%fused_computation.57 | loop fusion | flops 28311552 | bytes 38036608 | tf_op jit(solution)/shard_map/mul | solution.py:67
  47.2 0.1 collective-permute-start.2
  47.3 3.8 collective-permute-start.3
  51.1 8.1 %fusion.80 = (f32[144,127,128]{1,0,2:T(8,128)}, f32[144,127,128]{1,0,2:T(8,128)}) fusion(f32[144,128,128]{1,0,2:T(8,128)S(1)} %fusion.43), kind=kLoop, calls=%fused_computation.120 | loop fusion | bytes 37453824 | tf_op jit(solution)/shard_map/slice | solution.py:46
  59.2 0.0 collective-permute-done.2
  59.2 13.2 %fusion.36 = f32[144,128,128]{1,0,2:T(8,128)} fusion(f32[144,128,1]{1,0,2:T(8,128)S(1)} %collective-permute-done.3, f32[144,128,128]{1,0,2:T(8,128)S(1)} %fusion.43, f32[144,128,1]{1,0,2:T(8,128)S(1)} %collective-permute-done.2, f32[144,127,128]{1,0,2:T(8,128)} %get-tuple-element.27, f32[144,127,128]{1,0,2:T(8,128)} %get-tuple-element.26, ...), kind=kLoop, calls=%fused_computation.48 | loop fusion | flops 28311552 | bytes 38036608 | tf_op jit(solution)/shard_map/mul | solution.py:67
  72.4 0.9 fusion.79
  73.3 0.1 collective-permute-start.4
  73.4 0.0 slice-start.2
  73.4 3.8 collective-permute-start.5
  77.2 14.4 %fusion.78 = (f32[144,127,128]{1,0,2:T(8,128)}, f32[144,127,128]{1,0,2:T(8,128)}) fusion(f32[144,128,128]{1,0,2:T(8,128)} %fusion.36), kind=kLoop, calls=%fused_computation.118 | loop fusion | bytes 37453824 | tf_op jit(solution)/shard_map/slice | solution.py:46
  91.6 0.0 collective-permute-done.4
  91.6 0.0 collective-permute-done.5
  91.7 13.2 %fusion.29 = f32[144,128,128]{1,0,2:T(8,128)} fusion(f32[144,128,1]{1,0,2:T(8,128)S(1)} %collective-permute-done.5, f32[144,128,128]{1,0,2:T(8,128)S(1)} %bitcast.47, f32[144,128,1]{1,0,2:T(8,128)S(1)} %collective-permute-done.4, f32[144,127,128]{1,0,2:T(8,128)} %get-tuple-element.23, f32[144,127,128]{1,0,2:T(8,128)} %get-tuple-element.22, ...), kind=kLoop, calls=%fused_computation.39 | loop fusion | flops 28311552 | bytes 38036608 | tf_op jit(solution)/shard_map/mul | solution.py:67
  104.9 0.9 fusion.77
  105.8 0.1 collective-permute-start.6
  105.9 0.0 slice-start.4
  105.9 0.0 slice-start.5
  105.9 3.9 collective-permute-start.7
  109.9 14.4 %fusion.76 = (f32[144,127,128]{1,0,2:T(8,128)}, f32[144,127,128]{1,0,2:T(8,128)}) fusion(f32[144,128,128]{1,0,2:T(8,128)} %fusion.29), kind=kLoop, calls=%fused_computation.116 | loop fusion | bytes 37453824 | tf_op jit(solution)/shard_map/slice | solution.py:46
  124.3 13.2 %fusion.22 = f32[144,128,128]{1,0,2:T(8,128)} fusion(f32[144,128,1]{1,0,2:T(8,128)S(1)} %collective-permute-done.7, f32[144,128,128]{1,0,2:T(8,128)S(1)} %bitcast.49, f32[144,128,1]{1,0,2:T(8,128)S(1)} %collective-permute-done.6, f32[144,127,128]{1,0,2:T(8,128)} %get-tuple-element.19, f32[144,127,128]{1,0,2:T(8,128)} %get-tuple-element.18, ...), kind=kLoop, calls=%fused_computation.30 | loop fusion | flops 28311552 | bytes 38036608 | tf_op jit(solution)/shard_map/mul | solution.py:67
  137.5 0.9 fusion.75
  138.5 0.1 collective-permute-start.8
  138.5 3.8 collective-permute-start.9
  142.3 14.4 %fusion.74 = (f32[144,127,128]{1,0,2:T(8,128)}, f32[144,127,128]{1,0,2:T(8,128)}) fusion(f32[144,128,128]{1,0,2:T(8,128)} %fusion.22), kind=kLoop, calls=%fused_computation.114 | loop fusion | bytes 37453824 | tf_op jit(solution)/shard_map/slice | solution.py:46
  156.8 16.4 %fusion.15 = f32[144,128,128]{1,0,2:T(8,128)S(1)} fusion(f32[144,128,1]{1,0,2:T(8,128)S(1)} %collective-permute-done.9, f32[144,128,128]{1,0,2:T(8,128)} %fusion.22, f32[144,128,1]{1,0,2:T(8,128)S(1)} %collective-permute-done.8, f32[144,127,128]{1,0,2:T(8,128)} %get-tuple-element.15, f32[144,127,128]{1,0,2:T(8,128)} %get-tuple-element.14, ...), kind=kLoop, calls=%fused_computation.21 | loop fusion | flops 28311552 | bytes 38036608 | tf_op jit(solution)/shard_map/mul | solution.py:67
  173.2 0.1 collective-permute-start.10
  173.2 3.8 collective-permute-start.11
  177.1 8.1 %fusion.72 = (f32[144,127,128]{1,0,2:T(8,128)}, f32[144,127,128]{1,0,2:T(8,128)}) fusion(f32[144,128,128]{1,0,2:T(8,128)S(1)} %fusion.15), kind=kLoop, calls=%fused_computation.112 | loop fusion | bytes 37453824 | tf_op jit(solution)/shard_map/slice | solution.py:46
  185.2 0.0 collective-permute-done.10
  185.2 0.0 collective-permute-done.11
  185.2 13.1 %fusion.8 = f32[144,128,128]{1,0,2:T(8,128)} fusion(f32[144,128,1]{1,0,2:T(8,128)S(1)} %collective-permute-done.11, f32[144,128,128]{1,0,2:T(8,128)S(1)} %fusion.15, f32[144,128,1]{1,0,2:T(8,128)S(1)} %collective-permute-done.10, f32[144,127,128]{1,0,2:T(8,128)} %get-tuple-element.11, f32[144,127,128]{1,0,2:T(8,128)} %get-tuple-element.10, ...), kind=kLoop, calls=%fused_computation.12 | loop fusion | flops 28311552 | bytes 38036608 | tf_op jit(solution)/shard_map/mul | solution.py:67
  198.3 9.6 %copy.23 = f32[144,128,128]{2,0,1:T(8,128)} copy(f32[144,128,128]{1,0,2:T(8,128)} %fusion.8) | data formatting | bytes 18874368 | tf_op jit(solution)/shard_map/mul | solution.py:67
  207.9 0.0 copy-start.5
  207.9 5.6 %all-to-all-start = ((f32[144,128,128]{2,0,1:T(8,128)}), f32[144,128,128]{2,0,1:T(8,128)}, u32[]{:S(2)}, u32[]{:S(2)}) async-start(f32[144,128,128]{2,0,1:T(8,128)} %copy.23), calls=%async_computation | async-start | bytes 18874368 | tf_op jit(solution)/shard_map/all_to_all | solution.py:80
  213.6 0.5 fusion.52
  214.1 0.1 slice_reduce_fusion.2
  214.2 0.1 mul.415
  214.3 0.7 copy.25
  215.0 0.4 reshape.154
  215.4 0.1 fusion.59
  215.5 2.7 fusion.50
  218.2 4.8 convolution_select_fusion
  223.0 95.8 %all-to-all-done = f32[144,128,128]{2,0,1:T(8,128)} async-done(((f32[144,128,128]{2,0,1:T(8,128)}), f32[144,128,128]{2,0,1:T(8,128)}, u32[]{:S(2)}, u32[]{:S(2)}) %all-to-all-start) | async-done | bytes 9437216 | tf_op jit(solution)/shard_map/all_to_all | solution.py:80
  318.8 6.5 %copy.24 = f32[144,8,16,128]{3,2,0,1:T(8,128)S(1)} copy(f32[144,8,16,128]{3,0,2,1:T(8,128)} %bitcast.2) | data formatting | bytes 18874368 | tf_op jit(solution)/shard_map/all_to_all | solution.py:80
  325.3 7.5 %fusion.46 = f32[16,128]{1,0:T(8,128)S(1)} fusion(f32[8,144]{1,0:T(8,128)S(1)} %mul.415, f32[144,8,16,128]{3,0,2,1:T(8,128)} %bitcast.2), kind=kLoop, calls=%fused_computation.62 | loop fusion | flops 4716544 | bytes 9449984 | tf_op jit(solution)/shard_map/reduce_sum | solution.py:103
  332.9 46.4 %fusion.3 = f32[144,8,16,128]{3,1,2,0:T(8,128)S(1)} fusion(f32[1152,1152]{1,0:T(8,128)} %convolution_select_fusion, f32[144,8,16,128]{3,2,1,0:T(8,128)S(1)} %bitcast.52, f32[2048]{0:T(1024)S(1)} %dynamic-slice_bitcast_fusion, f32[2048]{0:T(1024)S(1)} %add_divide_fusion, f32[1152]{0:T(1024)S(1)} %get-tuple-element.7, f32[2048]{0:T(1024)S(1)} %get-tuple-element.35, ...), kind=kOutput, calls=%fused_computation.6 | convolution fusion | flops 32640860160 | bytes 24233984 | tf_op jit(solution)/shard_map/dot_general | solution.py:111
  379.3 2.3 copy.28
  381.5 107.8 %all_to_all.33 = f32[1152,16,128]{2,1,0:T(8,128)S(1)} all-to-all(f32[1152,16,128]{2,1,0:T(8,128)S(1)} %bitcast.50), channel_id=1, replica_groups=mesh['sector'=4,'group'=8] {'group'}, dimensions={0} | all-to-all | bytes 18874368 | tf_op jit(solution)/shard_map/all_to_all | solution.py:113
  489.3 5.2 %copy.26 = f32[8,144,16,128]{3,2,0,1:T(8,128)} copy(f32[8,144,16,128]{3,2,1,0:T(8,128)S(1)} %bitcast.51) | data formatting | bytes 18874368 | tf_op jit(solution)/shard_map/all_to_all | solution.py:113
  (40 shorter events, 0.2 us)
Async XLA Ops:
  0.0 30.1 %copy-start = (f32[32]{0:T(128)S(1)}, f32[32]{0:T(128)}, u32[]{:S(2)}) copy-start(f32[32]{0:T(128)} %param.13) | copy-start | bytes 388
  10.5 20.3 %collective-permute-start = (f32[144,128,1]{1,0,2:T(8,128)S(1)}, f32[144,128,1]{1,0,2:T(8,128)S(1)}, u32[]{:S(2)}, u32[]{:S(2)}) collective-permute-start(f32[144,128,1]{1,0,2:T(8,128)S(1)} %get-tuple-element.32), channel_id=1, source_target_pairs={{0,8},{8,16},{16,24},{24,0},{1,9},{9,17},{17,25},{25,1},{2,10},{10... | collective-permute-start | bytes 221192 | tf_op jit(solution)/shard_map/ppermute | solution.py:20
  13.6 17.2 %collective-permute-start.1 = (f32[144,128,1]{1,0,2:T(8,128)S(1)}, f32[144,128,1]{1,0,2:T(8,128)S(1)}, u32[]{:S(2)}, u32[]{:S(2)}) collective-permute-start(f32[144,128,1]{1,0,2:T(8,128)S(1)} %get-tuple-element.33), channel_id=1, source_target_pairs={{8,0},{16,8},{24,16},{0,24},{9,1},{17,9},{25,17},{1,25},{10,2},{18... | collective-permute-start | bytes 221192 | tf_op jit(solution)/shard_map/ppermute | solution.py:22
  15.8 14.3 %copy-start.4 = (s32[1152]{0:T(1024)S(1)}, s32[1152]{0:T(1024)}, u32[]{:S(2)}) copy-start(s32[1152]{0:T(1024)} %param.12) | copy-start | bytes 13828
  15.8 14.9 %copy-start.3 = (s32[128,128]{1,0:T(8,128)S(1)}, s32[128,128]{1,0:T(8,128)}, u32[]{:S(2)}) copy-start(s32[128,128]{1,0:T(8,128)} %param.10) | copy-start | bytes 196612
  47.2 12.0 %collective-permute-start.2 = (f32[144,128,1]{1,0,2:T(8,128)S(1)}, f32[144,128,1]{1,0,2:T(8,128)S(1)}, u32[]{:S(2)}, u32[]{:S(2)}) collective-permute-start(f32[144,128,1]{1,0,2:T(8,128)S(1)} %get-tuple-element.28), channel_id=1, source_target_pairs={{0,8},{8,16},{16,24},{24,0},{1,9},{9,17},{17,25},{25,1},{2,10},{10... | collective-permute-start | bytes 221192 | tf_op jit(solution)/shard_map/ppermute | solution.py:20
  47.3 11.9 %collective-permute-start.3 = (f32[144,128,1]{1,0,2:T(8,128)S(1)}, f32[144,128,1]{1,0,2:T(8,128)S(1)}, u32[]{:S(2)}, u32[]{:S(2)}) collective-permute-start(f32[144,128,1]{1,0,2:T(8,128)S(1)} %get-tuple-element.29), channel_id=1, source_target_pairs={{8,0},{16,8},{24,16},{0,24},{9,1},{17,9},{25,17},{1,25},{10,2},{18... | collective-permute-start | bytes 221192 | tf_op jit(solution)/shard_map/ppermute | solution.py:22
  73.3 18.3 %collective-permute-start.4 = (f32[144,128,1]{1,0,2:T(8,128)S(1)}, f32[144,128,1]{1,0,2:T(8,128)S(1)}, u32[]{:S(2)}, u32[]{:S(2)}) collective-permute-start(f32[144,128,1]{1,0,2:T(8,128)S(1)} %get-tuple-element.24), channel_id=1, source_target_pairs={{0,8},{8,16},{16,24},{24,0},{1,9},{9,17},{17,25},{25,1},{2,10},{10... | collective-permute-start | bytes 221192 | tf_op jit(solution)/shard_map/ppermute | solution.py:20
  73.4 18.2 %slice-start = ((s8[9437184]{0:T(1024)(128)(4,1)}), s8[4194304]{0:T(1024)(128)(4,1)S(1)}, s32[]{:S(2)}) async-start(s8[9437184]{0:T(1024)(128)(4,1)} %bitcast.46), calls=%async_computation.2 | async-start | bytes 8388608
  73.4 18.2 %slice-start.1 = ((s8[9437184]{0:T(1024)(128)(4,1)}), s8[4194304]{0:T(1024)(128)(4,1)S(1)}, s32[]{:S(2)}) async-start(s8[9437184]{0:T(1024)(128)(4,1)} %bitcast.46), calls=%async_computation.3 | async-start | bytes 8388608
  73.4 18.2 %slice-start.2 = ((s8[9437184]{0:T(1024)(128)(4,1)}), s8[1048576]{0:T(1024)(128)(4,1)S(1)}, s32[]{:S(2)}) async-start(s8[9437184]{0:T(1024)(128)(4,1)} %bitcast.46), calls=%async_computation.4 | async-start | bytes 2097152
  73.4 18.2 %collective-permute-start.5 = (f32[144,128,1]{1,0,2:T(8,128)S(1)}, f32[144,128,1]{1,0,2:T(8,128)S(1)}, u32[]{:S(2)}, u32[]{:S(2)}) collective-permute-start(f32[144,128,1]{1,0,2:T(8,128)S(1)} %get-tuple-element.25), channel_id=1, source_target_pairs={{8,0},{16,8},{24,16},{0,24},{9,1},{17,9},{25,17},{1,25},{10,2},{18... | collective-permute-start | bytes 221192 | tf_op jit(solution)/shard_map/ppermute | solution.py:22
  105.8 18.5 %collective-permute-start.6 = (f32[144,128,1]{1,0,2:T(8,128)S(1)}, f32[144,128,1]{1,0,2:T(8,128)S(1)}, u32[]{:S(2)}, u32[]{:S(2)}) collective-permute-start(f32[144,128,1]{1,0,2:T(8,128)S(1)} %get-tuple-element.20), channel_id=1, source_target_pairs={{0,8},{8,16},{16,24},{24,0},{1,9},{9,17},{17,25},{25,1},{2,10},{10... | collective-permute-start | bytes 221192 | tf_op jit(solution)/shard_map/ppermute | solution.py:20
  105.9 18.4 %slice-start.3 = ((s8[9437184]{0:T(1024)(128)(4,1)}), s8[4194304]{0:T(1024)(128)(4,1)S(1)}, s32[]{:S(2)}) async-start(s8[9437184]{0:T(1024)(128)(4,1)} %bitcast.48), calls=%async_computation.5 | async-start | bytes 8388608
  105.9 18.4 %slice-start.4 = ((s8[9437184]{0:T(1024)(128)(4,1)}), s8[4194304]{0:T(1024)(128)(4,1)S(1)}, s32[]{:S(2)}) async-start(s8[9437184]{0:T(1024)(128)(4,1)} %bitcast.48), calls=%async_computation.6 | async-start | bytes 8388608
  105.9 18.4 %slice-start.5 = ((s8[9437184]{0:T(1024)(128)(4,1)}), s8[1048576]{0:T(1024)(128)(4,1)S(1)}, s32[]{:S(2)}) async-start(s8[9437184]{0:T(1024)(128)(4,1)} %bitcast.48), calls=%async_computation.7 | async-start | bytes 2097152
  105.9 18.4 %collective-permute-start.7 = (f32[144,128,1]{1,0,2:T(8,128)S(1)}, f32[144,128,1]{1,0,2:T(8,128)S(1)}, u32[]{:S(2)}, u32[]{:S(2)}) collective-permute-start(f32[144,128,1]{1,0,2:T(8,128)S(1)} %get-tuple-element.21), channel_id=1, source_target_pairs={{8,0},{16,8},{24,16},{0,24},{9,1},{17,9},{25,17},{1,25},{10,2},{18... | collective-permute-start | bytes 221192 | tf_op jit(solution)/shard_map/ppermute | solution.py:22
  138.5 18.3 %collective-permute-start.8 = (f32[144,128,1]{1,0,2:T(8,128)S(1)}, f32[144,128,1]{1,0,2:T(8,128)S(1)}, u32[]{:S(2)}, u32[]{:S(2)}) collective-permute-start(f32[144,128,1]{1,0,2:T(8,128)S(1)} %get-tuple-element.16), channel_id=1, source_target_pairs={{0,8},{8,16},{16,24},{24,0},{1,9},{9,17},{17,25},{25,1},{2,10},{10... | collective-permute-start | bytes 221192 | tf_op jit(solution)/shard_map/ppermute | solution.py:20
  138.5 18.2 %collective-permute-start.9 = (f32[144,128,1]{1,0,2:T(8,128)S(1)}, f32[144,128,1]{1,0,2:T(8,128)S(1)}, u32[]{:S(2)}, u32[]{:S(2)}) collective-permute-start(f32[144,128,1]{1,0,2:T(8,128)S(1)} %get-tuple-element.17), channel_id=1, source_target_pairs={{8,0},{16,8},{24,16},{0,24},{9,1},{17,9},{25,17},{1,25},{10,2},{18... | collective-permute-start | bytes 221192 | tf_op jit(solution)/shard_map/ppermute | solution.py:22
  173.2 12.0 %collective-permute-start.10 = (f32[144,128,1]{1,0,2:T(8,128)S(1)}, f32[144,128,1]{1,0,2:T(8,128)S(1)}, u32[]{:S(2)}, u32[]{:S(2)}) collective-permute-start(f32[144,128,1]{1,0,2:T(8,128)S(1)} %get-tuple-element.12), channel_id=1, source_target_pairs={{0,8},{8,16},{16,24},{24,0},{1,9},{9,17},{17,25},{25,1},{2,10},{10... | collective-permute-start | bytes 221192 | tf_op jit(solution)/shard_map/ppermute | solution.py:20
  173.2 11.9 %collective-permute-start.11 = (f32[144,128,1]{1,0,2:T(8,128)S(1)}, f32[144,128,1]{1,0,2:T(8,128)S(1)}, u32[]{:S(2)}, u32[]{:S(2)}) collective-permute-start(f32[144,128,1]{1,0,2:T(8,128)S(1)} %get-tuple-element.13), channel_id=1, source_target_pairs={{8,0},{16,8},{24,16},{0,24},{9,1},{17,9},{25,17},{1,25},{10,2},{18... | collective-permute-start | bytes 221192 | tf_op jit(solution)/shard_map/ppermute | solution.py:22
  207.9 5.7 %copy-start.6 = (f32[32]{0:T(128)S(1)}, f32[32]{0:T(128)}, u32[]{:S(2)}) copy-start(f32[32]{0:T(128)} %param.16) | copy-start | bytes 388
  207.9 5.7 %copy-start.7 = (f32[32]{0:T(128)S(1)}, f32[32]{0:T(128)}, u32[]{:S(2)}) copy-start(f32[32]{0:T(128)} %param.15) | copy-start | bytes 388
  207.9 5.7 %copy-start.8 = (f32[32]{0:T(128)S(1)}, f32[32]{0:T(128)}, u32[]{:S(2)}) copy-start(f32[32]{0:T(128)} %param.14) | copy-start | bytes 388
  207.9 6.3 %copy-start.2 = (f32[32,36,36]{2,0,1:T(8,128)S(1)}, f32[32,36,36]{2,0,1:T(8,128)}, u32[]{:S(2)}) copy-start(f32[32,36,36]{2,0,1:T(8,128)} %param.17) | copy-start | bytes 497668
  207.9 7.5 %copy-start.5 = (f32[2,16,128]{2,1,0:T(8,128)S(1)}, f32[2,16,128]{2,1,0:T(8,128)}, u32[]{:S(2)}) copy-start(f32[2,16,128]{2,1,0:T(8,128)} %param.11) | copy-start | bytes 49156
  207.9 110.9 %all-to-all-start = ((f32[144,128,128]{2,0,1:T(8,128)}), f32[144,128,128]{2,0,1:T(8,128)}, u32[]{:S(2)}, u32[]{:S(2)}) async-start(f32[144,128,128]{2,0,1:T(8,128)} %copy.23), calls=%async_computation | async-start | bytes 18874368 | tf_op jit(solution)/shard_map/all_to_all | solution.py:80
  489.3 5.2 %copy-start.1 = (f32[32]{0:T(128)S(1)}, f32[32]{0:T(128)}, u32[]{:S(2)}) copy-start(f32[32]{0:T(128)} %param.13) | copy-start | bytes 388
where the time goes:
time: 503 us; the launch traced here: 495 us
  local copies, waits for them, and re-layouts  112 us (22%)
  blocking collectives  108 us (21%)
  waiting for transfers between devices  95.8 us (19%)
  other arithmetic  93.6 us (19%)
  matrix products  54.6 us (11%)
  starting transfers between devices  30.3 us (6%)
    all_to_all x1, blocking collectives, local(): lax.all_to_all(renewed.reshape(all_comps, rows_dev, lon_local), 'group',...  108 us
    all_to_all x1, waiting for transfers between devices, local(): lax.all_to_all(propagate(spectrum, flow_x, flow_y, sea_mask), 'group', sp...  95.8 us
    mul x6, other arithmetic, propagate(): combine(wave, padded[:, :, :-2], padded[:, :, 2:], rates) * sea_mask[None]  85.5 us
    slice x6, local copies, waits for them, and re-layouts, combine(): from_south = jnp.pad(centre[:, :-1], ((0, 0), (1, 0), (0, 0)))  73.7 us
    dot_general x1, matrix products, local(): mixed = jnp.dot(coupling, energy, precision=lax.Precision.HIGHEST)  46.4 us
    ppermute x6, starting transfers between devices, extended(): lax.ppermute(head, axis, [((i + 1) % count, i) for i in range(count)])  21.2 us
    unnamed x33, local copies, waits for them, and re-layouts  12.7 us
  transfers between devices with their start and end apart: 13, of which 1 were waited for; matrix products, arithmetic and copies ran while one was open for 17% of the time, Pallas kernels for 0%

commit v1 on v0

--- a/solution.py
+++ b/solution.py
@@ -8,6 +8,12 @@
 FREQ = 32
 SUBSTEPS = 6
 LAT = 128
+
+
+def trade_parts(x, name, split, join):
+    cells = jnp.split(x, lax.axis_size(name), axis=split)
+    arrived = lax.all_to_all(jnp.stack(cells), name, 0, 0)
+    return jnp.concatenate(arrived, axis=join)
 
 
 def extended(cells, sides, width):
@@ -110,13 +116,7 @@
     )
     mixed = jnp.dot(coupling, energy, precision=lax.Precision.HIGHEST)
     renewed = (energy * jnp.exp(exponent) + 0.5 * mixed) * sea_rows[None, :]
-    return lax.all_to_all(
-        renewed.reshape(all_comps, rows_dev, lon_local),
-        "group",
-        split_axis=0,
-        concat_axis=1,
-        tiled=True,
-    )
+    return trade_parts(renewed.reshape(all_comps, rows_dev, lon_local), "group", 0, 1)
 
 
 def solution(mesh):

time: 503 us -> 504 us (level)
    all_to_all x1 -> x0, local copies, waits for them, and re-layouts: 5.2 us -> none  [local(): lax.all_to_all(renewed.reshape(all_comps, rows_dev, lon_local), 'group',...]
    reshape x0 -> x1, local copies, waits for them, and re-layouts: none -> 5.2 us  [trade_parts(): return jnp.concatenate(arrived, axis=join)]
    unnamed x33 -> x48, local copies, waits for them, and re-layouts: 12.7 us -> 14 us
where the time goes in v1:
time: 504 us; the launch traced here: 496 us
  local copies, waits for them, and re-layouts  113 us (22%)
  blocking collectives  108 us (21%)
  waiting for transfers between devices  95.8 us (19%)
  other arithmetic  93.3 us (19%)
  matrix products  54.7 us (11%)
  starting transfers between devices  30.3 us (6%)
    all_to_all x1, blocking collectives, trade_parts(): arrived = lax.all_to_all(jnp.stack(cells), name, 0, 0)  108 us
    all_to_all x1, waiting for transfers between devices, local(): lax.all_to_all(propagate(spectrum, flow_x, flow_y, sea_mask), 'group', sp...  95.8 us
    mul x6, other arithmetic, propagate(): combine(wave, padded[:, :, :-2], padded[:, :, 2:], rates) * sea_mask[None]  85.2 us
    slice x6, local copies, waits for them, and re-layouts, combine(): from_south = jnp.pad(centre[:, :-1], ((0, 0), (1, 0), (0, 0)))  73.7 us
    dot_general x1, matrix products, local(): mixed = jnp.dot(coupling, energy, precision=lax.Precision.HIGHEST)  46.4 us
    ppermute x6, starting transfers between devices, extended(): lax.ppermute(head, axis, [((i + 1) % count, i) for i in range(count)])  21.2 us
    unnamed x48, local copies, waits for them, and re-layouts  14 us
  transfers between devices with their start and end apart: 13, of which 1 were waited for; matrix products, arithmetic and copies ran while one was open for 17% of the time, Pallas kernels for 0%

profile of v1, /device:TPU:0, one launch (start us, length us, event | category | flops | bytes accessed | tf_op | source)
XLA Modules:
  0.0 496.1 jit_solution(61934045604755149)
XLA Ops:
  0.0 9.6 %copy.15 = f32[144,128,128]{1,0,2:T(8,128)} copy(f32[144,128,128]{2,1,0:T(8,128)} %param.9) | data formatting | bytes 18874368 | tf_op args[0]
  9.6 0.9 fusion.82
  10.5 3.1 collective-permute-start
  13.6 2.1 collective-permute-start.1
  15.8 14.2 %fusion.81 = (f32[144,127,128]{1,0,2:T(8,128)}, f32[144,127,128]{1,0,2:T(8,128)}) fusion(f32[144,128,128]{1,0,2:T(8,128)} %copy.15), kind=kLoop, calls=%fused_computation.137 | loop fusion | bytes 37453824 | tf_op jit(solution)/shard_map/slice | solution.py:52
  30.0 0.1 and_select_fusion.1
  30.1 0.2 fusion.54
  30.3 0.2 fusion.69
  30.6 0.1 subtract_subtract_fusion
  30.7 0.1 copy.22
  30.8 16.4 %fusion.42 = f32[144,128,128]{1,0,2:T(8,128)S(1)} fusion(f32[144,128,1]{1,0,2:T(8,128)S(1)} %collective-permute-done.1, f32[144,128,128]{1,0,2:T(8,128)} %copy.15, f32[144,128,1]{1,0,2:T(8,128)S(1)} %collective-permute-done, f32[144,127,128]{1,0,2:T(8,128)} %get-tuple-element.39, f32[144,127,128]{1,0,2:T(8,128)} %get-tuple-element.38, ...), kind=kLoop, calls=%fused_computation.56 | loop fusion | flops 28311552 | bytes 38036608 | tf_op jit(solution)/shard_map/mul | solution.py:73
  47.2 0.1 collective-permute-start.2
  47.3 3.8 collective-permute-start.3
  51.1 8.1 %fusion.79 = (f32[144,127,128]{1,0,2:T(8,128)}, f32[144,127,128]{1,0,2:T(8,128)}) fusion(f32[144,128,128]{1,0,2:T(8,128)S(1)} %fusion.42), kind=kLoop, calls=%fused_computation.135 | loop fusion | bytes 37453824 | tf_op jit(solution)/shard_map/slice | solution.py:52
  59.2 13.1 %fusion.35 = f32[144,128,128]{1,0,2:T(8,128)} fusion(f32[144,128,1]{1,0,2:T(8,128)S(1)} %collective-permute-done.3, f32[144,128,128]{1,0,2:T(8,128)S(1)} %fusion.42, f32[144,128,1]{1,0,2:T(8,128)S(1)} %collective-permute-done.2, f32[144,127,128]{1,0,2:T(8,128)} %get-tuple-element.35, f32[144,127,128]{1,0,2:T(8,128)} %get-tuple-element.34, ...), kind=kLoop, calls=%fused_computation.47 | loop fusion | flops 28311552 | bytes 38036608 | tf_op jit(solution)/shard_map/mul | solution.py:73
  72.3 0.9 fusion.78
  73.2 0.1 collective-permute-start.4
  73.3 3.8 collective-permute-start.5
  77.1 14.4 %fusion.77 = (f32[144,127,128]{1,0,2:T(8,128)}, f32[144,127,128]{1,0,2:T(8,128)}) fusion(f32[144,128,128]{1,0,2:T(8,128)} %fusion.35), kind=kLoop, calls=%fused_computation.133 | loop fusion | bytes 37453824 | tf_op jit(solution)/shard_map/slice | solution.py:52
  91.6 13.1 %fusion.28 = f32[144,128,128]{1,0,2:T(8,128)} fusion(f32[144,128,1]{1,0,2:T(8,128)S(1)} %collective-permute-done.5, f32[144,128,128]{1,0,2:T(8,128)S(1)} %bitcast.88, f32[144,128,1]{1,0,2:T(8,128)S(1)} %collective-permute-done.4, f32[144,127,128]{1,0,2:T(8,128)} %get-tuple-element.31, f32[144,127,128]{1,0,2:T(8,128)} %get-tuple-element.30, ...), kind=kLoop, calls=%fused_computation.38 | loop fusion | flops 28311552 | bytes 38036608 | tf_op jit(solution)/shard_map/mul | solution.py:73
  104.7 0.9 fusion.76
  105.7 0.1 collective-permute-start.6
  105.8 3.9 collective-permute-start.7
  109.7 14.4 %fusion.75 = (f32[144,127,128]{1,0,2:T(8,128)}, f32[144,127,128]{1,0,2:T(8,128)}) fusion(f32[144,128,128]{1,0,2:T(8,128)} %fusion.28), kind=kLoop, calls=%fused_computation.131 | loop fusion | bytes 37453824 | tf_op jit(solution)/shard_map/slice | solution.py:52
  124.2 13.1 %fusion.21 = f32[144,128,128]{1,0,2:T(8,128)} fusion(f32[144,128,1]{1,0,2:T(8,128)S(1)} %collective-permute-done.7, f32[144,128,128]{1,0,2:T(8,128)S(1)} %bitcast.90, f32[144,128,1]{1,0,2:T(8,128)S(1)} %collective-permute-done.6, f32[144,127,128]{1,0,2:T(8,128)} %get-tuple-element.27, f32[144,127,128]{1,0,2:T(8,128)} %get-tuple-element.26, ...), kind=kLoop, calls=%fused_computation.29 | loop fusion | flops 28311552 | bytes 38036608 | tf_op jit(solution)/shard_map/mul | solution.py:73
  137.3 0.9 fusion.74
  138.3 3.8 collective-permute-start.9
  142.1 14.4 %fusion.73 = (f32[144,127,128]{1,0,2:T(8,128)}, f32[144,127,128]{1,0,2:T(8,128)}) fusion(f32[144,128,128]{1,0,2:T(8,128)} %fusion.21), kind=kLoop, calls=%fused_computation.129 | loop fusion | bytes 37453824 | tf_op jit(solution)/shard_map/slice | solution.py:52
  156.5 16.4 %fusion.14 = f32[144,128,128]{1,0,2:T(8,128)S(1)} fusion(f32[144,128,1]{1,0,2:T(8,128)S(1)} %collective-permute-done.9, f32[144,128,128]{1,0,2:T(8,128)} %fusion.21, f32[144,128,1]{1,0,2:T(8,128)S(1)} %collective-permute-done.8, f32[144,127,128]{1,0,2:T(8,128)} %get-tuple-element.23, f32[144,127,128]{1,0,2:T(8,128)} %get-tuple-element.22, ...), kind=kLoop, calls=%fused_computation.20 | loop fusion | flops 28311552 | bytes 38036608 | tf_op jit(solution)/shard_map/mul | solution.py:73
  173.0 3.8 collective-permute-start.11
  176.8 8.1 %fusion.71 = (f32[144,127,128]{1,0,2:T(8,128)}, f32[144,127,128]{1,0,2:T(8,128)}) fusion(f32[144,128,128]{1,0,2:T(8,128)S(1)} %fusion.14), kind=kLoop, calls=%fused_computation.127 | loop fusion | bytes 37453824 | tf_op jit(solution)/shard_map/slice | solution.py:52
  184.9 13.1 %fusion.7 = f32[144,128,128]{1,0,2:T(8,128)} fusion(f32[144,128,1]{1,0,2:T(8,128)S(1)} %collective-permute-done.11, f32[144,128,128]{1,0,2:T(8,128)S(1)} %fusion.14, f32[144,128,1]{1,0,2:T(8,128)S(1)} %collective-permute-done.10, f32[144,127,128]{1,0,2:T(8,128)} %get-tuple-element.19, f32[144,127,128]{1,0,2:T(8,128)} %get-tuple-element.18, ...), kind=kLoop, calls=%fused_computation.11 | loop fusion | flops 28311552 | bytes 38036608 | tf_op jit(solution)/shard_map/mul | solution.py:73
  198.0 9.6 %copy.23 = f32[144,128,128]{2,0,1:T(8,128)} copy(f32[144,128,128]{1,0,2:T(8,128)} %fusion.7) | data formatting | bytes 18874368 | tf_op jit(solution)/shard_map/mul | solution.py:73
  207.7 5.6 %all-to-all-start = ((f32[144,128,128]{2,0,1:T(8,128)}), f32[144,128,128]{2,0,1:T(8,128)}, u32[]{:S(2)}, u32[]{:S(2)}) async-start(f32[144,128,128]{2,0,1:T(8,128)} %copy.23), calls=%async_computation | async-start | bytes 18874368 | tf_op jit(solution)/shard_map/all_to_all | solution.py:86
  213.4 0.5 fusion.51
  213.9 0.1 mul.415
  214.0 0.7 copy.25
  214.8 0.4 reshape.174
  215.1 0.1 fusion.58
  215.2 2.7 fusion.49
  217.9 4.8 convolution_select_fusion
  222.8 95.8 %all-to-all-done = f32[144,128,128]{2,0,1:T(8,128)} async-done(((f32[144,128,128]{2,0,1:T(8,128)}), f32[144,128,128]{2,0,1:T(8,128)}, u32[]{:S(2)}, u32[]{:S(2)}) %all-to-all-start) | async-done | bytes 9437216 | tf_op jit(solution)/shard_map/all_to_all | solution.py:86
  318.6 6.5 %copy.24 = f32[144,8,16,128]{3,2,0,1:T(8,128)S(1)} copy(f32[144,8,16,128]{3,0,2,1:T(8,128)} %bitcast.2) | data formatting | bytes 18874368 | tf_op jit(solution)/shard_map/all_to_all | solution.py:86
  325.1 7.5 %fusion.45 = f32[16,128]{1,0:T(8,128)S(1)} fusion(f32[8,144]{1,0:T(8,128)S(1)} %mul.415, f32[144,8,16,128]{3,0,2,1:T(8,128)} %bitcast.2), kind=kLoop, calls=%fused_computation.61 | loop fusion | flops 4716544 | bytes 9449984 | tf_op jit(solution)/shard_map/reduce_sum | solution.py:109
  332.6 46.4 %fusion.2 = f32[1152,2048]{1,0:T(8,128)S(1)} fusion(f32[1152,1152]{1,0:T(8,128)} %convolution_select_fusion, f32[144,8,16,128]{3,2,1,0:T(8,128)S(1)} %bitcast.92, f32[2048]{0:T(1024)S(1)} %dynamic-slice_bitcast_fusion, f32[2048]{0:T(1024)S(1)} %add_divide_fusion, f32[1152]{0:T(1024)S(1)} %get-tuple-element.7, f32[2048]{0:T(1024)S(1)} %get-tuple-element.43, ...), kind=kOutput, calls=%fused_computation.5 | convolution fusion | flops 32640860160 | bytes 24233984 | tf_op jit(solution)/shard_map/dot_general | solution.py:117
  379.0 1.4 slice_bitcast_fusion
  380.4 0.2 copy.28
  380.6 0.1 bitcast_dynamic-update-slice_fusion.7
  380.7 0.2 copy.29
  380.9 0.2 copy.30
  381.2 0.2 copy.31
  381.4 0.2 copy.32
  381.6 0.2 copy.33
  381.8 0.2 copy.34
  382.0 0.2 copy.35
  382.2 0.1 bitcast_dynamic-update-slice_fusion.6
  382.3 0.1 bitcast_dynamic-update-slice_fusion.5
  382.4 0.1 bitcast_dynamic-update-slice_fusion.4
  382.5 0.1 bitcast_dynamic-update-slice_fusion.3
  382.6 0.1 bitcast_dynamic-update-slice_fusion.2
  382.7 0.1 bitcast_dynamic-update-slice_fusion.1
  382.8 0.1 bitcast_dynamic-update-slice_fusion
  382.8 107.8 %all_to_all.20 = f32[8,144,16,128]{3,2,1,0:T(8,128)S(1)} all-to-all(f32[8,144,16,128]{3,2,1,0:T(8,128)S(1)} %bitcast_dynamic-update-slice_fusion), channel_id=1, replica_groups=mesh['sector'=4,'group'=8] {'group'}, dimensions={0} | all-to-all | bytes 18874368 | tf_op jit(solution)/shard_map/all_to_all | solution.py:15
  490.7 5.2 %copy.26 = f32[144,8,16,128]{3,2,1,0:T(8,128)} copy(f32[144,8,16,128]{3,2,0,1:T(8,128)S(1)} %bitcast.91) | data formatting | bytes 18874368 | tf_op jit(solution)/shard_map/reshape | solution.py:16
  (56 shorter events, 0.4 us)
Async XLA Ops:
  0.0 30.1 %copy-start = (f32[32]{0:T(128)S(1)}, f32[32]{0:T(128)}, u32[]{:S(2)}) copy-start(f32[32]{0:T(128)} %param.13) | copy-start | bytes 388
  10.5 20.3 %collective-permute-start = (f32[144,128,1]{1,0,2:T(8,128)S(1)}, f32[144,128,1]{1,0,2:T(8,128)S(1)}, u32[]{:S(2)}, u32[]{:S(2)}) collective-permute-start(f32[144,128,1]{1,0,2:T(8,128)S(1)} %get-tuple-element.40), channel_id=1, source_target_pairs={{0,8},{8,16},{16,24},{24,0},{1,9},{9,17},{17,25},{25,1},{2,10},{10... | collective-permute-start | bytes 221192 | tf_op jit(solution)/shard_map/ppermute | solution.py:26
  13.6 17.2 %collective-permute-start.1 = (f32[144,128,1]{1,0,2:T(8,128)S(1)}, f32[144,128,1]{1,0,2:T(8,128)S(1)}, u32[]{:S(2)}, u32[]{:S(2)}) collective-permute-start(f32[144,128,1]{1,0,2:T(8,128)S(1)} %get-tuple-element.41), channel_id=1, source_target_pairs={{8,0},{16,8},{24,16},{0,24},{9,1},{17,9},{25,17},{1,25},{10,2},{18... | collective-permute-start | bytes 221192 | tf_op jit(solution)/shard_map/ppermute | solution.py:28
  15.8 14.3 %copy-start.4 = (s32[1152]{0:T(1024)S(1)}, s32[1152]{0:T(1024)}, u32[]{:S(2)}) copy-start(s32[1152]{0:T(1024)} %param.12) | copy-start | bytes 13828
  15.8 14.9 %copy-start.3 = (s32[128,128]{1,0:T(8,128)S(1)}, s32[128,128]{1,0:T(8,128)}, u32[]{:S(2)}) copy-start(s32[128,128]{1,0:T(8,128)} %param.10) | copy-start | bytes 196612
  47.2 12.0 %collective-permute-start.2 = (f32[144,128,1]{1,0,2:T(8,128)S(1)}, f32[144,128,1]{1,0,2:T(8,128)S(1)}, u32[]{:S(2)}, u32[]{:S(2)}) collective-permute-start(f32[144,128,1]{1,0,2:T(8,128)S(1)} %get-tuple-element.36), channel_id=1, source_target_pairs={{0,8},{8,16},{16,24},{24,0},{1,9},{9,17},{17,25},{25,1},{2,10},{10... | collective-permute-start | bytes 221192 | tf_op jit(solution)/shard_map/ppermute | solution.py:26
  47.3 11.9 %collective-permute-start.3 = (f32[144,128,1]{1,0,2:T(8,128)S(1)}, f32[144,128,1]{1,0,2:T(8,128)S(1)}, u32[]{:S(2)}, u32[]{:S(2)}) collective-permute-start(f32[144,128,1]{1,0,2:T(8,128)S(1)} %get-tuple-element.37), channel_id=1, source_target_pairs={{8,0},{16,8},{24,16},{0,24},{9,1},{17,9},{25,17},{1,25},{10,2},{18... | collective-permute-start | bytes 221192 | tf_op jit(solution)/shard_map/ppermute | solution.py:28
  73.2 18.3 %collective-permute-start.4 = (f32[144,128,1]{1,0,2:T(8,128)S(1)}, f32[144,128,1]{1,0,2:T(8,128)S(1)}, u32[]{:S(2)}, u32[]{:S(2)}) collective-permute-start(f32[144,128,1]{1,0,2:T(8,128)S(1)} %get-tuple-element.32), channel_id=1, source_target_pairs={{0,8},{8,16},{16,24},{24,0},{1,9},{9,17},{17,25},{25,1},{2,10},{10... | collective-permute-start | bytes 221192 | tf_op jit(solution)/shard_map/ppermute | solution.py:26
  73.3 18.2 %slice-start = ((s8[9437184]{0:T(1024)(128)(4,1)}), s8[4194304]{0:T(1024)(128)(4,1)S(1)}, s32[]{:S(2)}) async-start(s8[9437184]{0:T(1024)(128)(4,1)} %bitcast.87), calls=%async_computation.2 | async-start | bytes 8388608
  73.3 18.2 %slice-start.1 = ((s8[9437184]{0:T(1024)(128)(4,1)}), s8[4194304]{0:T(1024)(128)(4,1)S(1)}, s32[]{:S(2)}) async-start(s8[9437184]{0:T(1024)(128)(4,1)} %bitcast.87), calls=%async_computation.3 | async-start | bytes 8388608
  73.3 18.2 %slice-start.2 = ((s8[9437184]{0:T(1024)(128)(4,1)}), s8[1048576]{0:T(1024)(128)(4,1)S(1)}, s32[]{:S(2)}) async-start(s8[9437184]{0:T(1024)(128)(4,1)} %bitcast.87), calls=%async_computation.4 | async-start | bytes 2097152
  73.3 18.2 %collective-permute-start.5 = (f32[144,128,1]{1,0,2:T(8,128)S(1)}, f32[144,128,1]{1,0,2:T(8,128)S(1)}, u32[]{:S(2)}, u32[]{:S(2)}) collective-permute-start(f32[144,128,1]{1,0,2:T(8,128)S(1)} %get-tuple-element.33), channel_id=1, source_target_pairs={{8,0},{16,8},{24,16},{0,24},{9,1},{17,9},{25,17},{1,25},{10,2},{18... | collective-permute-start | bytes 221192 | tf_op jit(solution)/shard_map/ppermute | solution.py:28
  105.7 18.5 %collective-permute-start.6 = (f32[144,128,1]{1,0,2:T(8,128)S(1)}, f32[144,128,1]{1,0,2:T(8,128)S(1)}, u32[]{:S(2)}, u32[]{:S(2)}) collective-permute-start(f32[144,128,1]{1,0,2:T(8,128)S(1)} %get-tuple-element.28), channel_id=1, source_target_pairs={{0,8},{8,16},{16,24},{24,0},{1,9},{9,17},{17,25},{25,1},{2,10},{10... | collective-permute-start | bytes 221192 | tf_op jit(solution)/shard_map/ppermute | solution.py:26
  105.7 18.4 %slice-start.3 = ((s8[9437184]{0:T(1024)(128)(4,1)}), s8[4194304]{0:T(1024)(128)(4,1)S(1)}, s32[]{:S(2)}) async-start(s8[9437184]{0:T(1024)(128)(4,1)} %bitcast.89), calls=%async_computation.5 | async-start | bytes 8388608
  105.7 18.4 %slice-start.4 = ((s8[9437184]{0:T(1024)(128)(4,1)}), s8[4194304]{0:T(1024)(128)(4,1)S(1)}, s32[]{:S(2)}) async-start(s8[9437184]{0:T(1024)(128)(4,1)} %bitcast.89), calls=%async_computation.6 | async-start | bytes 8388608
  105.7 18.4 %slice-start.5 = ((s8[9437184]{0:T(1024)(128)(4,1)}), s8[1048576]{0:T(1024)(128)(4,1)S(1)}, s32[]{:S(2)}) async-start(s8[9437184]{0:T(1024)(128)(4,1)} %bitcast.89), calls=%async_computation.7 | async-start | bytes 2097152
  105.8 18.4 %collective-permute-start.7 = (f32[144,128,1]{1,0,2:T(8,128)S(1)}, f32[144,128,1]{1,0,2:T(8,128)S(1)}, u32[]{:S(2)}, u32[]{:S(2)}) collective-permute-start(f32[144,128,1]{1,0,2:T(8,128)S(1)} %get-tuple-element.29), channel_id=1, source_target_pairs={{8,0},{16,8},{24,16},{0,24},{9,1},{17,9},{25,17},{1,25},{10,2},{18... | collective-permute-start | bytes 221192 | tf_op jit(solution)/shard_map/ppermute | solution.py:28
  138.2 18.3 %collective-permute-start.8 = (f32[144,128,1]{1,0,2:T(8,128)S(1)}, f32[144,128,1]{1,0,2:T(8,128)S(1)}, u32[]{:S(2)}, u32[]{:S(2)}) collective-permute-start(f32[144,128,1]{1,0,2:T(8,128)S(1)} %get-tuple-element.24), channel_id=1, source_target_pairs={{0,8},{8,16},{16,24},{24,0},{1,9},{9,17},{17,25},{25,1},{2,10},{10... | collective-permute-start | bytes 221192 | tf_op jit(solution)/shard_map/ppermute | solution.py:26
  138.3 18.2 %collective-permute-start.9 = (f32[144,128,1]{1,0,2:T(8,128)S(1)}, f32[144,128,1]{1,0,2:T(8,128)S(1)}, u32[]{:S(2)}, u32[]{:S(2)}) collective-permute-start(f32[144,128,1]{1,0,2:T(8,128)S(1)} %get-tuple-element.25), channel_id=1, source_target_pairs={{8,0},{16,8},{24,16},{0,24},{9,1},{17,9},{25,17},{1,25},{10,2},{18... | collective-permute-start | bytes 221192 | tf_op jit(solution)/shard_map/ppermute | solution.py:28
  172.9 12.0 %collective-permute-start.10 = (f32[144,128,1]{1,0,2:T(8,128)S(1)}, f32[144,128,1]{1,0,2:T(8,128)S(1)}, u32[]{:S(2)}, u32[]{:S(2)}) collective-permute-start(f32[144,128,1]{1,0,2:T(8,128)S(1)} %get-tuple-element.20), channel_id=1, source_target_pairs={{0,8},{8,16},{16,24},{24,0},{1,9},{9,17},{17,25},{25,1},{2,10},{10... | collective-permute-start | bytes 221192 | tf_op jit(solution)/shard_map/ppermute | solution.py:26
  173.0 11.9 %collective-permute-start.11 = (f32[144,128,1]{1,0,2:T(8,128)S(1)}, f32[144,128,1]{1,0,2:T(8,128)S(1)}, u32[]{:S(2)}, u32[]{:S(2)}) collective-permute-start(f32[144,128,1]{1,0,2:T(8,128)S(1)} %get-tuple-element.21), channel_id=1, source_target_pairs={{8,0},{16,8},{24,16},{0,24},{9,1},{17,9},{25,17},{1,25},{10,2},{18... | collective-permute-start | bytes 221192 | tf_op jit(solution)/shard_map/ppermute | solution.py:28
  207.7 5.7 %copy-start.6 = (f32[32]{0:T(128)S(1)}, f32[32]{0:T(128)}, u32[]{:S(2)}) copy-start(f32[32]{0:T(128)} %param.16) | copy-start | bytes 388
  207.7 5.7 %copy-start.7 = (f32[32]{0:T(128)S(1)}, f32[32]{0:T(128)}, u32[]{:S(2)}) copy-start(f32[32]{0:T(128)} %param.15) | copy-start | bytes 388
  207.7 5.7 %copy-start.8 = (f32[32]{0:T(128)S(1)}, f32[32]{0:T(128)}, u32[]{:S(2)}) copy-start(f32[32]{0:T(128)} %param.14) | copy-start | bytes 388
  207.7 6.3 %copy-start.2 = (f32[32,36,36]{2,0,1:T(8,128)S(1)}, f32[32,36,36]{2,0,1:T(8,128)}, u32[]{:S(2)}) copy-start(f32[32,36,36]{2,0,1:T(8,128)} %param.17) | copy-start | bytes 497668
  207.7 7.5 %copy-start.5 = (f32[2,16,128]{2,1,0:T(8,128)S(1)}, f32[2,16,128]{2,1,0:T(8,128)}, u32[]{:S(2)}) copy-start(f32[2,16,128]{2,1,0:T(8,128)} %param.11) | copy-start | bytes 49156
  207.7 110.9 %all-to-all-start = ((f32[144,128,128]{2,0,1:T(8,128)}), f32[144,128,128]{2,0,1:T(8,128)}, u32[]{:S(2)}, u32[]{:S(2)}) async-start(f32[144,128,128]{2,0,1:T(8,128)} %copy.23), calls=%async_computation | async-start | bytes 18874368 | tf_op jit(solution)/shard_map/all_to_all | solution.py:86
  490.7 5.2 %copy-start.1 = (f32[32]{0:T(128)S(1)}, f32[32]{0:T(128)}, u32[]{:S(2)}) copy-start(f32[32]{0:T(128)} %param.13) | copy-start | bytes 388
